TPU v7x, 512 devices: a whole 4x4x16 slice. The times are simulated.
512 devices in a mesh: dp: 8 (over x_hi, y), fsdp: 64 (over z, x_lo, core).
Axes of the slice: x: 4 (x_hi: 2, x_lo: 2; x = x_hi * 2 + x_lo), y: 4, z: 16, core: 2. Of those that a mesh axis runs over, the one named last changes fastest.
Arguments:
- samples: bfloat16 [1024, 256, 768], P(('dp', 'fsdp')), may hold values from -6 to 6
- cotangent: bfloat16 [1024, 256, 768], P(('dp', 'fsdp')), may hold values from -6 to 6
- w_in: bfloat16 [3072, 768], P('fsdp'), may hold values from -0.21875 to 0.21875
- w_out: bfloat16 [3072, 768], P('fsdp'), may hold values from -0.21875 to 0.21875
- sketch_in: bfloat16 [768, 16], replicated, may hold values from -0.21875 to 0.21875
- sketch_hidden: bfloat16 [3072, 16], replicated, may hold values from -0.109375 to 0.109375
- targets: float32 [1024], P(('dp', 'fsdp')), may hold values from -6 to 6
Outputs:
- coeffs: float32 [1024], P(('dp', 'fsdp'))
- sketched_step: float32 [512], replicated
All inputs are finite; a program needn't handle non-finite values.
Results may differ from a plain program's by a relative error of at most 0.0054.
Values may be sent and summed in bfloat16 or wider, within the bound.
A program may use at most 64 MiB of HBM per device.

v0:
```python
import jax
import jax.numpy as jnp
from jax import lax
from jax.sharding import PartitionSpec as P

DAMPING = 0.5


def per_device(samples, cotangent, w_in, w_out, sketch_in, sketch_hidden, targets):
    count, length, width = samples.shape
    flat_x = samples.reshape(count * length, width)
    flat_g = cotangent.reshape(count * length, width)
    rows_in = lax.all_gather(w_in, "fsdp", axis=0, tiled=True)
    rows_out = lax.all_gather(w_out, "fsdp", axis=0, tiled=True)
    all_targets = lax.all_gather(targets, ("dp", "fsdp"), axis=0, tiled=True)
    pre = lax.dot_general(
        flat_x, rows_in, (((1,), (1,)), ((), ())), preferred_element_type=jnp.float32
    )
    back = lax.dot_general(
        flat_g, rows_out, (((1,), (1,)), ((), ())), preferred_element_type=jnp.float32
    )
    sig = jax.nn.sigmoid(pre)
    hidden = (pre * sig).astype(jnp.bfloat16)
    slope = (back * sig * (1.0 + pre * (1.0 - sig))).astype(jnp.bfloat16)
    hq = jnp.dot(hidden, sketch_hidden, preferred_element_type=jnp.float32)
    dq = jnp.dot(slope, sketch_hidden, preferred_element_type=jnp.float32)
    xp = jnp.dot(flat_x, sketch_in, preferred_element_type=jnp.float32)
    gp = jnp.dot(flat_g, sketch_in, preferred_element_type=jnp.float32)

    def outer(left, right):
        return (
            jnp.einsum(
                "spr,spq->srq",
                left.reshape(count, length, -1),
                right.reshape(count, length, -1),
                precision=lax.Precision.HIGHEST,
            )
            / length
        ).reshape(count, -1)

    feats = jnp.concatenate([outer(dq, xp), outer(hq, gp)], axis=1).astype(jnp.bfloat16)
    everyone = lax.all_gather(feats, ("dp", "fsdp"), axis=0, tiled=True)
    size = feats.shape[1]
    small = lax.dot_general(
        everyone, everyone, (((0,), (0,)), ((), ())), preferred_element_type=jnp.float32
    )
    right = lax.dot_general(
        everyone.astype(jnp.float32),
        all_targets,
        (((0,), (0,)), ((), ())),
        precision=lax.Precision.HIGHEST,
    )
    factor = jnp.linalg.cholesky(small + DAMPING * jnp.eye(size, dtype=jnp.float32))
    step = jax.scipy.linalg.cho_solve((factor, True), right)
    fitted = jnp.dot(feats.astype(jnp.float32), step, precision=lax.Precision.HIGHEST)
    coeffs = (targets - fitted) / DAMPING
    return (coeffs, step)


def solution(mesh):
    in_specs = (
        P(("dp", "fsdp"), None, None),
        P(("dp", "fsdp"), None, None),
        P("fsdp", None),
        P("fsdp", None),
        P(),
        P(),
        P(("dp", "fsdp")),
    )
    out_specs = (P(("dp", "fsdp")), P())
    return jax.shard_map(
        per_device, mesh=mesh, in_specs=in_specs, out_specs=out_specs, check_vma=False
    )
```

profile of v0, /device:TPU:1, one launch (start us, length us, event | category | flops | bytes accessed | tf_op | source)
XLA Modules:
  0.0 1186.7 jit_solution(7681346825893043996)
XLA Ops:
  8.7 1.0 fusion.46
  9.8 1.5 fusion.44
  11.2 129.1 %all-gather.7.cloned.1.call-done = bf16[3072,768]{1,0:T(8,128)(2,1)} async-done(((bf16[48,768]{1,0:T(8,128)(2,1)}), bf16[3072,768]{1,0:T(8,128)(2,1)}) %all-gather.7.cloned.1.call-update) | async-done | bytes 4718608 | tf_op jit(solution)/shard_map/all_gather | solution.py:13
  140.3 4.6 fusion.74
  144.9 2.6 copy-done.9
  147.5 1.9 fusion
  149.4 113.7 %all-gather.5.cloned.1.call-done = bf16[3072,768]{1,0:T(8,128)(2,1)} async-done(((bf16[48,768]{1,0:T(8,128)(2,1)}), bf16[3072,768]{1,0:T(8,128)(2,1)}) %all-gather.5.cloned.1.call-update) | async-done | bytes 4718608 | tf_op jit(solution)/shard_map/all_gather | solution.py:14
  263.1 8.1 fusion.1
  272.6 102.0 %all-reduce.1 = f32[1024]{0:T(1024)S(1)} all-reduce(f32[1024]{0:T(1024)S(1)} %dynamic-update-slice.23), channel_id=1, replica_groups=mesh['dp'=8,'fsdp'=64] {'dp','fsdp'}, use_global_device_ids=true, to_apply=%add.1 | all-reduce | flops 1024 | bytes 8192
  374.6 661.0 %all-gather.9.cloned.1.call-done = bf16[512,2,512]{2,1,0:T(2,128)(2,1)} async-done(((bf16[1,2,512]{2,1,0:T(2,128)(2,1)}), bf16[512,2,512]{2,1,0:T(2,128)(2,1)}) %all-gather.9.cloned.1.call-update) | async-done | bytes 1048592 | tf_op jit(solution)/shard_map/all_gather | solution.py:42
  1035.7 1.6 reshape.169
  1037.3 1.0 copy-done.1
  1038.3 0.7 fusion.75
  1039.6 1.0 copy-done.2
  1040.7 11.7 cholesky.103
  1052.5 9.8 custom-call.34
  1062.4 1.2 constant_dynamic-update-slice_fusion.5
  1063.6 1.3 convolution_subtract_fusion
  1064.9 11.7 cholesky.215
  1076.6 10.0 custom-call.35
  1086.9 1.3 convolution_subtract_fusion.1
  1088.2 11.7 cholesky.236
  1100.6 9.8 custom-call.36
  1110.6 1.2 convolution_subtract_fusion.2
  1111.9 11.9 %cholesky.253 = f32[128,128]{1,0:T(8,128)S(1)} custom-call(f32[128,128]{1,0:T(8,128)S(1)} %convolution_subtract_fusion.2), custom_call_target="Cholesky" | custom-call | tf_op jit(solution)/shard_map/jit(cholesky)/cholesky | solution.py:53
  1127.7 7.7 while.1
  1128.4 1.3 bitcast_dynamic-update-slice_fusion.2
  1130.3 1.3 bitcast_dynamic-update-slice_fusion.2
  1132.2 1.3 bitcast_dynamic-update-slice_fusion.2
  1134.1 1.3 bitcast_dynamic-update-slice_fusion.2
  1135.4 39.3 %custom-call.37 = f32[4,128,128]{1,2,0:T(8,128)S(1)} custom-call(f32[4,128,128]{2,1,0:T(8,128)S(1)} %get-tuple-element.9), custom_call_target="InvertDiagBlocksLowerTriangular" | custom-call | tf_op jit(solution)/shard_map/jit(_cho_solve)/triangular_solve | solution.py:54
  1174.7 1.7 fusion.76
  (74 shorter events, 12.5 us)
Async XLA Ops:
  7.2 1.5 copy-start
  7.2 133.1 %all-gather.7.cloned.1.call-start = ((), (), s32[]{:S(2)}) async-start(), calls=%async_computation.1 | async-start | bytes 4792320 | tf_op jit(solution)/shard_map/all_gather | solution.py:13
  7.9 255.2 %all-gather.5.cloned.1.call-start = ((), (), s32[]{:S(2)}) async-start(), calls=%async_computation | async-start | bytes 4792320 | tf_op jit(solution)/shard_map/all_gather | solution.py:14
  8.7 1027.0 %all-gather.9.cloned.1.call-start = ((), (), s32[]{:S(2)}) async-start(), calls=%async_computation.2 | async-start | bytes 1050624 | tf_op jit(solution)/shard_map/all_gather | solution.py:42
  140.3 7.2 copy-start.7
  144.8 2.7 copy-start.9
  147.5 115.6 %copy-start.3 = (bf16[2,256,768]{2,1,0:T(8,128)(2,1)S(1)}, bf16[2,256,768]{2,1,0:T(8,128)(2,1)}, u32[]{:S(2)}) copy-start(bf16[2,256,768]{2,1,0:T(8,128)(2,1)} %param.8) | copy-start | bytes 2359300
  263.1 9.3 copy-start.8
  271.7 0.6 copy-start.4
  1037.3 1.0 copy-start.1
  1039.4 140.1 %copy-start.5 = (bf16[2,512]{1,0:T(2,128)(2,1)S(1)}, bf16[2,512]{1,0:T(2,128)(2,1)}, u32[]{:S(2)}) copy-start(bf16[2,512]{1,0:T(2,128)(2,1)} %copy-done.4) | copy-start | bytes 6148
  1039.6 1.0 copy-start.2
  1179.5 0.7 copy-start.6
Sparse Core Ops, SparseCore 0:
  10.1 130.0 all-gather.6
  142.4 120.6 all-gather.4
  272.4 763.1 all-gather.8
where the time goes:
time: 1190 us
  waiting for transfers between devices  905 us (76%)
  other arithmetic  118 us (10%)
  blocking collectives  102 us (9%)
  matrix products  28.8 us (2%)
  between operations  16.5 us (1%)
  local copies, waits for them, and re-layouts  15.5 us (1%)
    all_gather x1, waiting for transfers between devices, per_device(): everyone = lax.all_gather(feats, ('dp', 'fsdp'), axis=0, tiled=True)  661 us
    all_gather x1, waiting for transfers between devices, per_device(): rows_in = lax.all_gather(w_in, 'fsdp', axis=0, tiled=True)  129 us
    all_gather x1, waiting for transfers between devices, per_device(): rows_out = lax.all_gather(w_out, 'fsdp', axis=0, tiled=True)  114 us
    unnamed x1, blocking collectives  102 us
    another operation x14, other arithmetic, per_device(): jnp.linalg.cholesky(small + DAMPING * jnp.eye(size, dtype=jnp.float32))  78.8 us
    another operation x4, other arithmetic, per_device(): step = jax.scipy.linalg.cho_solve((factor, True), right)  39.5 us
  transfers between devices with their start and end apart: 3, of which 3 were waited for; matrix products, arithmetic and copies ran while one was open for 1% of the time, Pallas kernels for 0%

commit v1 on v0

--- a/solution.py
+++ b/solution.py
@@ -39,7 +39,10 @@
         ).reshape(count, -1)
 
     feats = jnp.concatenate([outer(dq, xp), outer(hq, gp)], axis=1).astype(jnp.bfloat16)
-    everyone = lax.all_gather(feats, ("dp", "fsdp"), axis=0, tiled=True)
+    everyone = jnp.concatenate(
+        lax.all_to_all(jnp.stack([feats] * lax.axis_size(("dp", "fsdp"))), ("dp", "fsdp"), 0, 0),
+        axis=0,
+    )
     size = feats.shape[1]
     small = lax.dot_general(
         everyone, everyone, (((0,), (0,)), ((), ())), preferred_element_type=jnp.float32

time: 1190 us -> 566 us (0.48)
  waiting for transfers between devices: 905 us -> 244 us
  blocking collectives: 102 us -> 119 us
  starting transfers between devices: 0.11 us -> 14.9 us
    all_gather x1 -> x0, waiting for transfers between devices: 661 us -> none  [per_device(): everyone = lax.all_gather(feats, ('dp', 'fsdp'), axis=0, tiled=True)]
    unnamed x1, blocking collectives: 102 us -> 119 us
    all_to_all x0 -> x1, starting transfers between devices: none -> 14.8 us  [per_device(): lax.all_to_all(jnp.stack([feats] * lax.axis_size(('dp', 'fsdp'))), ('dp',...]
  transfers between devices with their start and end apart: 3 -> 3, of which waited for: 3 -> 2; matrix products, arithmetic and copies ran while one was open for 1% -> 2% of each run, Pallas kernels for 0% -> 0%
where the time goes in v1:
time: 566 us; the launch traced here: 558 us
  waiting for transfers between devices  244 us (43%)
  blocking collectives  119 us (21%)
  other arithmetic  118 us (21%)
  matrix products  27.6 us (5%)
  local copies, waits for them, and re-layouts  17.1 us (3%)
  between operations  17.1 us (3%)
  starting transfers between devices  14.9 us (3%)
    all_gather x1, waiting for transfers between devices, per_device(): rows_in = lax.all_gather(w_in, 'fsdp', axis=0, tiled=True)  129 us
    unnamed x1, blocking collectives  119 us
    all_gather x1, waiting for transfers between devices, per_device(): rows_out = lax.all_gather(w_out, 'fsdp', axis=0, tiled=True)  114 us
    another operation x14, other arithmetic, per_device(): jnp.linalg.cholesky(small + DAMPING * jnp.eye(size, dtype=jnp.float32))  78.8 us
    another operation x4, other arithmetic, per_device(): step = jax.scipy.linalg.cho_solve((factor, True), right)  39.5 us
    all_to_all x1, starting transfers between devices, per_device(): lax.all_to_all(jnp.stack([feats] * lax.axis_size(('dp', 'fsdp'))), ('dp',...  14.8 us
  transfers between devices with their start and end apart: 3, of which 2 were waited for; matrix products, arithmetic and copies ran while one was open for 2% of the time, Pallas kernels for 0%

profile of v1, /device:TPU:1, one launch (start us, length us, event | category | flops | bytes accessed | tf_op | source)
XLA Modules:
  0.0 558.1 jit_solution(4656263926337969756)
XLA Ops:
  8.7 1.0 fusion.47
  9.7 1.5 fusion.45
  11.2 129.1 %all-gather.5.cloned.1.call-done = bf16[3072,768]{1,0:T(8,128)(2,1)} async-done(((bf16[48,768]{1,0:T(8,128)(2,1)}), bf16[3072,768]{1,0:T(8,128)(2,1)}) %all-gather.5.cloned.1.call-update) | async-done | bytes 4718608 | tf_op jit(solution)/shard_map/all_gather | solution.py:13
  140.3 4.6 fusion.75
  144.9 2.7 copy-done.7
  147.5 1.9 fusion
  149.4 113.7 %all-gather.3.cloned.1.call-done = bf16[3072,768]{1,0:T(8,128)(2,1)} async-done(((bf16[48,768]{1,0:T(8,128)(2,1)}), bf16[3072,768]{1,0:T(8,128)(2,1)}) %all-gather.3.cloned.1.call-update) | async-done | bytes 4718608 | tf_op jit(solution)/shard_map/all_gather | solution.py:14
  263.1 8.1 %fusion.1 = f32[512,16]{0,1:T(8,128)S(1)} fusion(bf16[3072,16]{0,1:T(8,128)(2,1)S(1)} %copy-done.5, f32[512,3072]{1,0:T(8,128)} %copy-done.7, bf16[512,768]{1,0:T(8,128)(2,1)S(1)} %bitcast.180, bf16[3072,768]{1,0:T(8,128)(2,1)} %all-gather.3.cloned.1.call-done), kind=kOutput, calls=%fused_computation.6 | convolution fusion | flops 2480406528 | bytes 11927552 | tf_op jit(solution)/shard_map/dot_general | solution.py:26
  271.7 1.5 stack.2
  273.3 14.8 %all-to-all-start = ((bf16[512,2,512]{2,1,0:T(2,128)(2,1)}), bf16[512,2,512]{2,1,0:T(2,128)(2,1)S(1)}, u32[]{:S(2)}, u32[]{:S(2)}) async-start(bf16[512,2,512]{2,1,0:T(2,128)(2,1)} %stack.2), calls=%async_computation | async-start | bytes 2097152 | tf_op jit(solution)/shard_map/all_to_all | solution.py:43
  288.4 118.7 %all-reduce.1 = f32[1024]{0:T(1024)S(1)} all-reduce(f32[1024]{0:T(1024)S(1)} %dynamic-update-slice.23), channel_id=1, replica_groups=mesh['dp'=8,'fsdp'=64] {'dp','fsdp'}, use_global_device_ids=true, to_apply=%add.1 | all-reduce | flops 1024 | bytes 8192
  407.1 1.0 copy-done.1
  408.1 0.7 convolution_bitcast_fusion
  409.4 1.0 copy-done.2
  410.5 11.7 %cholesky.103 = f32[128,128]{1,0:T(8,128)S(1)} custom-call(f32[128,128]{1,0:T(8,128)S(1)} %cholesky.263), custom_call_target="Cholesky" | custom-call | tf_op jit(solution)/shard_map/jit(cholesky)/cholesky | solution.py:56
  422.3 9.8 %custom-call.34 = f32[1,128,128]{1,2,0:T(8,128)S(1)} custom-call(f32[1,128,128]{2,1,0:T(8,128)S(1)} %get-tuple-element.29), custom_call_target="InvertDiagBlocksLowerTriangular" | custom-call | tf_op jit(solution)/shard_map/jit(cholesky)/cholesky | solution.py:56
  432.2 1.2 constant_dynamic-update-slice_fusion.5
  433.4 1.3 convolution_subtract_fusion
  434.7 11.7 %cholesky.215 = f32[128,128]{1,0:T(8,128)S(1)} custom-call(f32[128,128]{1,0:T(8,128)S(1)} %cholesky.267), custom_call_target="Cholesky" | custom-call | tf_op jit(solution)/shard_map/jit(cholesky)/cholesky | solution.py:56
  446.4 10.0 %custom-call.35 = f32[1,128,128]{1,2,0:T(8,128)S(1)} custom-call(f32[1,128,128]{2,1,0:T(8,128)S(1)} %get-tuple-element.26), custom_call_target="InvertDiagBlocksLowerTriangular" | custom-call | tf_op jit(solution)/shard_map/jit(cholesky)/cholesky | solution.py:56
  456.7 1.3 convolution_subtract_fusion.1
  458.0 11.7 %cholesky.236 = f32[128,128]{1,0:T(8,128)S(1)} custom-call(f32[128,128]{1,0:T(8,128)S(1)} %cholesky.272), custom_call_target="Cholesky" | custom-call | tf_op jit(solution)/shard_map/jit(cholesky)/cholesky | solution.py:56
  470.4 9.8 %custom-call.36 = f32[1,128,128]{1,2,0:T(8,128)S(1)} custom-call(f32[1,128,128]{2,1,0:T(8,128)S(1)} %get-tuple-element.23), custom_call_target="InvertDiagBlocksLowerTriangular" | custom-call | tf_op jit(solution)/shard_map/jit(cholesky)/cholesky | solution.py:56
  480.4 1.2 convolution_subtract_fusion.2
  481.6 11.9 %cholesky.253 = f32[128,128]{1,0:T(8,128)S(1)} custom-call(f32[128,128]{1,0:T(8,128)S(1)} %convolution_subtract_fusion.2), custom_call_target="Cholesky" | custom-call | tf_op jit(solution)/shard_map/jit(cholesky)/cholesky | solution.py:56
  497.6 8.5 %while.1 = (s32[]{:T(128)}, f32[512,512]{1,0:T(8,128)S(1)}, s32[4,2]{0,1:T(2,128)S(1)}, f32[4,128,128]{2,1,0:T(8,128)S(1)}, s32[]{:T(128)}) while((s32[]{:T(128)}, f32[512,512]{1,0:T(8,128)S(1)}, s32[4,2]{0,1:T(2,128)S(1)}, f32[4,128,128]{2,1,0:T(8,128)S(1)}, s32[]{:T(128)}) %tuple.31), condition=%wide.while_cond, body=%wide.while_body.sunk | while | flops 2 | bytes 131181 | solution.py:57
  498.3 1.4 bitcast_dynamic-update-slice_fusion.2
  500.4 1.4 bitcast_dynamic-update-slice_fusion.2
  502.5 1.4 bitcast_dynamic-update-slice_fusion.2
  504.6 1.4 bitcast_dynamic-update-slice_fusion.2
  506.1 39.3 %custom-call.37 = f32[4,128,128]{1,2,0:T(8,128)S(1)} custom-call(f32[4,128,128]{2,1,0:T(8,128)S(1)} %get-tuple-element.9), custom_call_target="InvertDiagBlocksLowerTriangular" | custom-call | tf_op jit(solution)/shard_map/jit(_cho_solve)/triangular_solve | solution.py:57
  545.4 1.5 reshape.155
  (70 shorter events, 12.5 us)
Async XLA Ops:
  7.2 1.5 copy-start
  7.2 133.1 %all-gather.5.cloned.1.call-start = ((), (), s32[]{:S(2)}) async-start(), calls=%async_computation.2 | async-start | bytes 4792320 | tf_op jit(solution)/shard_map/all_gather | solution.py:13
  7.9 255.2 %all-gather.3.cloned.1.call-start = ((), (), s32[]{:S(2)}) async-start(), calls=%async_computation.1 | async-start | bytes 4792320 | tf_op jit(solution)/shard_map/all_gather | solution.py:14
  140.3 7.2 %copy-start.5 = (bf16[3072,16]{0,1:T(8,128)(2,1)S(1)}, bf16[3072,16]{0,1:T(8,128)(2,1)}, u32[]{:S(2)}) copy-start(bf16[3072,16]{0,1:T(8,128)(2,1)} %param.12) | copy-start | bytes 294916
  144.8 2.7 copy-start.7
  147.5 115.6 %copy-start.3 = (bf16[2,256,768]{2,1,0:T(8,128)(2,1)S(1)}, bf16[2,256,768]{2,1,0:T(8,128)(2,1)}, u32[]{:S(2)}) copy-start(bf16[2,256,768]{2,1,0:T(8,128)(2,1)} %param.8) | copy-start | bytes 2359300
  263.1 25.0 %copy-start.6 = (f32[2]{0:T(128)S(1)}, f32[2]{0:T(128)}, u32[]{:S(2)}) copy-start(f32[2]{0:T(128)} %param.13) | copy-start | bytes 28
  273.3 133.8 %all-to-all-start = ((bf16[512,2,512]{2,1,0:T(2,128)(2,1)}), bf16[512,2,512]{2,1,0:T(2,128)(2,1)S(1)}, u32[]{:S(2)}, u32[]{:S(2)}) async-start(bf16[512,2,512]{2,1,0:T(2,128)(2,1)} %stack.2), calls=%async_computation | async-start | bytes 2097152 | tf_op jit(solution)/shard_map/all_to_all | solution.py:43
  407.1 1.0 copy-start.1
  409.4 1.0 copy-start.2
  550.3 0.7 copy-start.4
Sparse Core Ops, SparseCore 0:
  10.1 130.0 all-gather.4
  142.4 120.6 all-gather.2
